TPU v7x, 256 devices: a whole 4x4x8 slice. The times are simulated.
256 devices in a mesh: energy: 64 (over z, x, core), sector: 4 (over y).
Axes of the slice: x: 4, y: 4, z: 8, core: 2. Of those that a mesh axis runs over, the one named last changes fastest.
Arguments:
- boundary: float32 [128, 2, 1024, 128], P('energy'), may hold values from -6 to 6
- energies: float32 [128], P('energy'), may hold values from 0.5 to 1.5
- levels: int32 [1024], replicated, may hold values from 0 to 31
- pattern: int32 [8, 8, 8], P('sector'), may hold values 0 or 1
- coupling: bfloat16 [8, 64, 128, 128], P('sector', 'energy'), may hold values from -0.125 to 0.125
Outputs:
- edge_state: float32 [4, 128, 2, 1024, 128], P('sector', 'energy')
All inputs are finite; a program needn't handle non-finite values. No bound on the sum of `pattern` on one device may be relied on, other than what follows from the above.
Results may differ from a plain program's by a relative error of at most 0.0003.
Values may be sent and summed in bfloat16 or wider, within the bound.
No kernel may reach another device: no remote copies, remote signals or barrier semaphores. Data moves between devices by JAX's collectives and lax.ppermute only.
A program may use at most 64 MiB of HBM per device.

v0:
```python
import jax
import jax.numpy as jnp
from jax import lax
from jax.sharding import Mesh
from jax.sharding import PartitionSpec as P

STEPS = 4
ENERGY = ("energy_0", "energy_1", "energy_2")


def in_order(tiles, dim):
    tiles = jnp.moveaxis(tiles, 0, dim)
    dims = tiles.shape
    return tiles.reshape(*dims[:dim], dims[dim] * dims[dim + 1], *dims[dim + 2 :])


def gather_in_order(x, axes, order):
    tiles = x[None]
    for k in order:
        tiles = lax.all_gather(tiles, axes[k], axis=0, tiled=True)
    held = [lax.axis_size(axes[k]) for k in reversed(order)]
    tiles = tiles.reshape(*held, *x.shape)
    turned = sorted(range(len(order)), key=lambda place: order[len(order) - 1 - place])
    return tiles.transpose(*turned, *range(len(order), tiles.ndim)).reshape(-1, *x.shape)


def gathered_by_axis(x, axes, order, dim):
    return in_order(gather_in_order(x, axes, order), dim)


def shifted(value, axis, steps):
    count = lax.axis_size(axis)
    leading, last = (max(0, -steps), min(count, count - steps))
    return lax.ppermute(value, axis, [(source, source + steps) for source in range(leading, last)])


def body(boundary, energies, levels, pattern, coupling):
    runs = lax.axis_size("sector")
    index = lax.axis_index("sector")
    sec_dev = coupling.shape[0]
    blocks_side = pattern.shape[1]
    width = coupling.shape[2]
    channels = blocks_side * width
    columns = boundary.shape[3]
    step_len = 1.6 / (sec_dev * STEPS * runs)
    gathered = gathered_by_axis(coupling, ENERGY, (1, 0, 2), 1)
    shaped = gathered.reshape(sec_dev, blocks_side, blocks_side, width, width)
    masked = shaped * pattern.astype(jnp.bfloat16)[:, :, :, None, None]
    thresholds = 0.05 * levels.astype(jnp.float32)

    def advance(state, energy_values):
        count = state.shape[0]
        diag_terms = thresholds[None, :, None] - energy_values[:, None, None]
        field = state[:, 0]
        slope = state[:, 1]
        for inner in range(sec_dev):
            for step in range(STEPS):
                low = field.astype(jnp.bfloat16).reshape(count, blocks_side, width, columns)
                coupled = jnp.einsum(
                    "ijab,ejbc->eiac", masked[inner], low, preferred_element_type=jnp.float32
                )
                coupled = coupled.reshape(count, channels, columns)
                slope = slope + step_len * (diag_terms * field + coupled)
                field = field + step_len * slope
        return jnp.stack([field, slope], axis=1)

    def keepsame(state, energy_values):
        return state

    count = energies.shape[0]

    def tick(tick_index, carry):
        received, result = carry
        slot = tick_index - index
        live = jnp.logical_and(slot >= 0, slot < count)
        where_at = jnp.clip(slot, 0, count - 1)
        own = lax.dynamic_slice_in_dim(boundary, where_at, 1, 0)
        energy_now = lax.dynamic_slice_in_dim(energies, where_at, 1, 0)
        start = jnp.where(index == 0, own, received)
        moved = lax.cond(live, advance, keepsame, start, energy_now)
        current = lax.dynamic_slice_in_dim(result, where_at, 1, 0)
        result = lax.dynamic_update_slice_in_dim(
            result, jnp.where(live, moved, current), where_at, 0
        )
        received = shifted(moved, "sector", 1)
        return (received, result)

    first = jnp.zeros_like(boundary[:1])
    received, result = lax.fori_loop(0, runs + count - 1, tick, (first, jnp.zeros_like(boundary)))
    return result[None]


def solution(mesh):
    split = Mesh(
        mesh.devices.reshape(8, 4, 2, mesh.shape["sector"]),
        ("energy_0", "energy_1", "energy_2", "sector"),
    )
    placed = (
        P(ENERGY, None, None, None),
        P(ENERGY),
        P(),
        P("sector", None, None),
        P("sector", ENERGY, None, None),
    )
    return jax.shard_map(
        body,
        mesh=split,
        in_specs=placed,
        out_specs=P("sector", ENERGY, None, None, None),
        check_vma=False,
    )
```

profile of v0, /device:TPU:24, one launch (start us, length us, event | category | flops | bytes accessed | tf_op | source)
XLA Modules:
  0.0 287.6 jit_solution(7945603454623909311)
XLA Ops:
  6.5 14.3 %all-gather = bf16[8,1,128,128]{3,2,1,0:T(8,128)(2,1)} all-gather(bf16[2,1,128,128]{3,2,1,0:T(8,128)(2,1)} %param.13), channel_id=2, replica_groups=mesh['energy_0'=8,'energy_1'=4,'energy_2'=2,'sector'=4] {'energy_1'}, dimensions={0}, use_global_device_ids=true | all-gather | bytes 327680 | tf_op jit(solution)/shard_map/all_gather | solution.py:20
  20.9 42.4 %all-gather.4.cloned.1.call-done = bf16[32,2,1,128,128]{4,3,2,1,0:T(8,128)(2,1)} async-done(((bf16[4,2,1,128,128]{4,3,2,1,0:T(8,128)(2,1)}), bf16[32,2,1,128,128]{4,3,2,1,0:T(8,128)(2,1)}) %all-gather.4.cloned.1.call-update) | async-done | bytes 2097168 | tf_op jit(solution)/shard_map/all_gather | solution.py:20
  63.4 19.3 %all-gather.6.cloned.1.call-done = bf16[64,2,1,128,128]{4,3,2,1,0:T(8,128)(2,1)} async-done(((bf16[32,2,1,128,128]{4,3,2,1,0:T(8,128)(2,1)}), bf16[64,2,1,128,128]{4,3,2,1,0:T(8,128)(2,1)}) %all-gather.6.cloned.1.call-update) | async-done | bytes 4194320 | tf_op jit(solution)/shard_map/all_gather | solution.py:20
  82.7 2.7 copy.11
  85.4 2.3 copy_multiply_fusion
  87.8 1.5 broadcast_in_dim.16
  89.3 191.5 %while.16 = (s32[]{:T(128)}, f32[1,2,1024,128]{3,2,1,0:T(8,128)S(1)}, f32[2,2,1024,128]{3,2,1,0:T(8,128)}, s32[]{:T(128)}, pred[]{:T(512)}, /*index=5*/f32[2,2,1...) while((s32[]{:T(128)}, ...), condition=%wide.region_3.4_spmd, body=%wide.region_0.3_spmd.sunk | while | flops 2166753280 | bytes 80532288 | solution.py:89
  89.3 1.3 dynamic-slice_select_fusion.2
  90.6 1.3 collective-permute-start
  91.9 2.3 select_dynamic-update-slice_fusion.2
  94.2 23.6 %collective-permute-done = f32[1,2,1024,128]{3,2,1,0:T(8,128)S(1)} collective-permute-done((f32[1,2,1024,128]{3,2,1,0:T(8,128)S(1)}, f32[1,2,1024,128]{3,2,1,0:T(8,128)S(1)}, u32[]{:S(2)}, u32[]{:S(2)}) %collective-permute-start) | collective-permute-done | bytes 1048608 | tf_op jit(solution)/shard_map/while/body/eval_jaxpr/ppermute | solution.py:34
  117.9 1.3 dynamic-slice_select_fusion.2
  119.2 1.3 collective-permute-start
  120.5 2.3 select_dynamic-update-slice_fusion.2
  122.8 22.8 %collective-permute-done = f32[1,2,1024,128]{3,2,1,0:T(8,128)S(1)} collective-permute-done((f32[1,2,1024,128]{3,2,1,0:T(8,128)S(1)}, f32[1,2,1024,128]{3,2,1,0:T(8,128)S(1)}, u32[]{:S(2)}, u32[]{:S(2)}) %collective-permute-start) | collective-permute-done | bytes 1048608 | tf_op jit(solution)/shard_map/while/body/eval_jaxpr/ppermute | solution.py:34
  145.6 1.3 dynamic-slice_select_fusion.2
  147.0 1.3 collective-permute-start
  148.3 2.3 select_dynamic-update-slice_fusion.2
  150.6 54.1 %collective-permute-done = f32[1,2,1024,128]{3,2,1,0:T(8,128)S(1)} collective-permute-done((f32[1,2,1024,128]{3,2,1,0:T(8,128)S(1)}, f32[1,2,1024,128]{3,2,1,0:T(8,128)S(1)}, u32[]{:S(2)}, u32[]{:S(2)}) %collective-permute-start) | collective-permute-done | bytes 1048608 | tf_op jit(solution)/shard_map/while/body/eval_jaxpr/ppermute | solution.py:34
  204.7 1.3 dynamic-slice_select_fusion.2
  206.0 11.7 %conditional.2 = (f32[1,2,1024,128]{3,2,1,0:T(8,128)S(1)}) conditional(s32[]{:T(128)} %convert_element_type.107, f32[1,2,1024,128]{3,2,1,0:T(8,128)S(1)} %dynamic-slice_select_fusion.2, (f32[1,2,1024,128]{3,2,1,0:T(8,128)S(1)}, f32[2]{0:T(128)S(1)}, s32[]{:T(128)}, f32[1024]{0:T(1024)S(1)}, bf16[2,8,8,128,128]{4,3,2,1,0:T(8,128)(2,1)}) %tuple.51), branch_computations={%region_1.1_spmd, %region_2.2_spmd} | conditional | flops 2166228992 | bytes 70045752 | solution.py:80
  208.1 2.4 fusion.14
  216.4 0.9 multiply_add_fusion
  217.7 1.3 collective-permute-start
  219.0 2.3 select_dynamic-update-slice_fusion.2
  221.3 21.9 %collective-permute-done = f32[1,2,1024,128]{3,2,1,0:T(8,128)S(1)} collective-permute-done((f32[1,2,1024,128]{3,2,1,0:T(8,128)S(1)}, f32[1,2,1024,128]{3,2,1,0:T(8,128)S(1)}, u32[]{:S(2)}, u32[]{:S(2)}) %collective-permute-start) | collective-permute-done | bytes 1048608 | tf_op jit(solution)/shard_map/while/body/eval_jaxpr/ppermute | solution.py:34
  243.2 1.3 dynamic-slice_select_fusion.2
  244.5 11.7 %conditional.2 = (f32[1,2,1024,128]{3,2,1,0:T(8,128)S(1)}) conditional(s32[]{:T(128)} %convert_element_type.107, f32[1,2,1024,128]{3,2,1,0:T(8,128)S(1)} %dynamic-slice_select_fusion.2, (f32[1,2,1024,128]{3,2,1,0:T(8,128)S(1)}, f32[2]{0:T(128)S(1)}, s32[]{:T(128)}, f32[1024]{0:T(1024)S(1)}, bf16[2,8,8,128,128]{4,3,2,1,0:T(8,128)(2,1)}) %tuple.51), branch_computations={%region_1.1_spmd, %region_2.2_spmd} | conditional | flops 2166228992 | bytes 70045752 | solution.py:80
  246.6 2.5 fusion.14
  256.2 1.3 collective-permute-start
  257.5 2.3 select_dynamic-update-slice_fusion.2
  259.8 21.0 %collective-permute-done = f32[1,2,1024,128]{3,2,1,0:T(8,128)S(1)} collective-permute-done((f32[1,2,1024,128]{3,2,1,0:T(8,128)S(1)}, f32[1,2,1024,128]{3,2,1,0:T(8,128)S(1)}, u32[]{:S(2)}, u32[]{:S(2)}) %collective-permute-start) | collective-permute-done | bytes 1048608 | tf_op jit(solution)/shard_map/while/body/eval_jaxpr/ppermute | solution.py:34
  (49 shorter events, 17.5 us)
Async XLA Ops:
  6.5 56.8 %copy-start.1 = (s32[2,8,8]{2,1,0:T(8,128)S(1)}, s32[2,8,8]{2,1,0:T(8,128)}, u32[]{:S(2)}) copy-start(s32[2,8,8]{2,1,0:T(8,128)} %param.12) | copy-start | bytes 1540
  6.5 56.9 %copy-start.2 = (s32[1024]{0:T(1024)S(1)}, s32[1024]{0:T(1024)}, u32[]{:S(2)}) copy-start(s32[1024]{0:T(1024)} %param.11) | copy-start | bytes 12292
  6.5 56.8 %all-gather.4.cloned.1.call-start = ((), (), s32[]{:S(2)}) async-start(), calls=%async_computation | async-start | bytes 2359296 | tf_op jit(solution)/shard_map/all_gather | solution.py:20
  20.9 61.8 %all-gather.6.cloned.1.call-start = ((), (), s32[]{:S(2)}) async-start(), calls=%async_computation.1 | async-start | bytes 6291456 | tf_op jit(solution)/shard_map/all_gather | solution.py:20
  87.7 1.5 copy-start.3
  90.6 27.2 %collective-permute-start = (f32[1,2,1024,128]{3,2,1,0:T(8,128)S(1)}, f32[1,2,1024,128]{3,2,1,0:T(8,128)S(1)}, u32[]{:S(2)}, u32[]{:S(2)}) collective-permute-start(f32[1,2,1024,128]{3,2,1,0:T(8,128)S(1)} %get-tuple-element.329), channel_id=1, source_target_pairs={{0,1},{1,2},{2,3},{4,5},{5,6},{6,7},{8,9},{9,10},{10,11},{12,13},{... | collective-permute-start | bytes 3145736 | tf_op jit(solution)/shard_map/while/body/eval_jaxpr/ppermute | solution.py:34
  119.2 26.4 %collective-permute-start = (f32[1,2,1024,128]{3,2,1,0:T(8,128)S(1)}, f32[1,2,1024,128]{3,2,1,0:T(8,128)S(1)}, u32[]{:S(2)}, u32[]{:S(2)}) collective-permute-start(f32[1,2,1024,128]{3,2,1,0:T(8,128)S(1)} %get-tuple-element.329), channel_id=1, source_target_pairs={{0,1},{1,2},{2,3},{4,5},{5,6},{6,7},{8,9},{9,10},{10,11},{12,13},{... | collective-permute-start | bytes 3145736 | tf_op jit(solution)/shard_map/while/body/eval_jaxpr/ppermute | solution.py:34
  147.0 57.7 %collective-permute-start = (f32[1,2,1024,128]{3,2,1,0:T(8,128)S(1)}, f32[1,2,1024,128]{3,2,1,0:T(8,128)S(1)}, u32[]{:S(2)}, u32[]{:S(2)}) collective-permute-start(f32[1,2,1024,128]{3,2,1,0:T(8,128)S(1)} %get-tuple-element.329), channel_id=1, source_target_pairs={{0,1},{1,2},{2,3},{4,5},{5,6},{6,7},{8,9},{9,10},{10,11},{12,13},{... | collective-permute-start | bytes 3145736 | tf_op jit(solution)/shard_map/while/body/eval_jaxpr/ppermute | solution.py:34
  208.1 2.8 copy-start
  217.7 25.5 %collective-permute-start = (f32[1,2,1024,128]{3,2,1,0:T(8,128)S(1)}, f32[1,2,1024,128]{3,2,1,0:T(8,128)S(1)}, u32[]{:S(2)}, u32[]{:S(2)}) collective-permute-start(f32[1,2,1024,128]{3,2,1,0:T(8,128)S(1)} %get-tuple-element.329), channel_id=1, source_target_pairs={{0,1},{1,2},{2,3},{4,5},{5,6},{6,7},{8,9},{9,10},{10,11},{12,13},{... | collective-permute-start | bytes 3145736 | tf_op jit(solution)/shard_map/while/body/eval_jaxpr/ppermute | solution.py:34
  246.6 2.8 copy-start
  256.2 24.6 %collective-permute-start = (f32[1,2,1024,128]{3,2,1,0:T(8,128)S(1)}, f32[1,2,1024,128]{3,2,1,0:T(8,128)S(1)}, u32[]{:S(2)}, u32[]{:S(2)}) collective-permute-start(f32[1,2,1024,128]{3,2,1,0:T(8,128)S(1)} %get-tuple-element.329), channel_id=1, source_target_pairs={{0,1},{1,2},{2,3},{4,5},{5,6},{6,7},{8,9},{9,10},{10,11},{12,13},{... | collective-permute-start | bytes 3145736 | tf_op jit(solution)/shard_map/while/body/eval_jaxpr/ppermute | solution.py:34
Sparse Core Ops, SparseCore 0:
  21.0 42.2 all-gather.3
  65.1 17.5 all-gather.5
where the time goes:
time: 288 us
  waiting for transfers between devices  205 us (71%)
  other arithmetic  25.6 us (9%)
  matrix products  15.9 us (6%)
  blocking collectives  14.3 us (5%)
  between operations  13.5 us (5%)
  starting transfers between devices  6.5 us (2%)
  local copies, waits for them, and re-layouts  6.31 us (2%)
    ppermute x5, waiting for transfers between devices, shifted(): lax.ppermute(value, axis, [(source, source + steps) for source in range(l...  143 us
    all_gather x2, waiting for transfers between devices, gather_in_order(): tiles = lax.all_gather(tiles, axes[k], axis=0, tiled=True)  61.7 us
    dot_general x16, matrix products, advance(): jnp.einsum('ijab,ejbc->eiac', masked[inner], low, preferred_element_type=...  15.9 us
    all_gather x1, blocking collectives, gather_in_order(): tiles = lax.all_gather(tiles, axes[k], axis=0, tiled=True)  14.3 us
    dynamic_update_slice x5, other arithmetic, tick(): lax.dynamic_update_slice_in_dim(result, jnp.where(live, moved, current),...  11.5 us
    select_n x5, other arithmetic, tick(): start = jnp.where(index == 0, own, received)  6.64 us
    ppermute x5, starting transfers between devices, shifted(): lax.ppermute(value, axis, [(source, source + steps) for source in range(l...  6.46 us
  transfers between devices with their start and end apart: 7, of which 7 were waited for; matrix products, arithmetic and copies ran while one was open for 4% of the time, Pallas kernels for 0%

commit v1 on v0

--- a/solution.py
+++ b/solution.py
@@ -17,7 +17,9 @@
 def gather_in_order(x, axes, order):
     tiles = x[None]
     for k in order:
-        tiles = lax.all_gather(tiles, axes[k], axis=0, tiled=True)
+        tiles = jnp.concatenate(
+            lax.all_to_all(jnp.stack([tiles] * lax.axis_size(axes[k])), axes[k], 0, 0), axis=0
+        )
     held = [lax.axis_size(axes[k]) for k in reversed(order)]
     tiles = tiles.reshape(*held, *x.shape)
     turned = sorted(range(len(order)), key=lambda place: order[len(order) - 1 - place])

time: 288 us -> 275 us (0.955)
  between operations: 13.5 us -> 0.07 us
  waiting for transfers between devices: 205 us -> 192 us
  starting transfers between devices: 6.5 us -> 15.1 us
  blocking collectives: 14.3 us -> 17.9 us
    all_gather x2 -> x0, waiting for transfers between devices: 61.7 us -> none  [gather_in_order(): tiles = lax.all_gather(tiles, axes[k], axis=0, tiled=True)]
    all_to_all x0 -> x1, waiting for transfers between devices: none -> 49.8 us  [gather_in_order(): lax.all_to_all(jnp.stack([tiles] * lax.axis_size(axes[k])), axes[k], 0, 0)]
    all_to_all x0 -> x2, blocking collectives: none -> 17.9 us  [gather_in_order(): lax.all_to_all(jnp.stack([tiles] * lax.axis_size(axes[k])), axes[k], 0, 0)]
    all_gather x1 -> x0, blocking collectives: 14.3 us -> none  [gather_in_order(): tiles = lax.all_gather(tiles, axes[k], axis=0, tiled=True)]
    all_to_all x0 -> x1, starting transfers between devices: none -> 8.6 us  [gather_in_order(): lax.all_to_all(jnp.stack([tiles] * lax.axis_size(axes[k])), axes[k], 0, 0)]
    another operation x0 -> x4, local copies, waits for them, and re-layouts: none -> 3.29 us  [gather_in_order(): jnp.stack([tiles] * lax.axis_size(axes[k]))]
  transfers between devices with their start and end apart: 7 -> 6, of which waited for: 7 -> 6; matrix products, arithmetic and copies ran while one was open for 4% -> 4% of each run, Pallas kernels for 0% -> 0%
where the time goes in v1:
time: 275 us
  waiting for transfers between devices  192 us (70%)
  other arithmetic  25.8 us (9%)
  blocking collectives  17.9 us (7%)
  matrix products  16.1 us (6%)
  starting transfers between devices  15.1 us (5%)
  local copies, waits for them, and re-layouts  7.34 us (3%)
    ppermute x5, waiting for transfers between devices, shifted(): lax.ppermute(value, axis, [(source, source + steps) for source in range(l...  142 us
    all_to_all x1, waiting for transfers between devices, gather_in_order(): lax.all_to_all(jnp.stack([tiles] * lax.axis_size(axes[k])), axes[k], 0, 0)  49.8 us
    all_to_all x2, blocking collectives, gather_in_order(): lax.all_to_all(jnp.stack([tiles] * lax.axis_size(axes[k])), axes[k], 0, 0)  17.9 us
    dot_general x16, matrix products, advance(): jnp.einsum('ijab,ejbc->eiac', masked[inner], low, preferred_element_type=...  16.1 us
    dynamic_update_slice x5, other arithmetic, tick(): lax.dynamic_update_slice_in_dim(result, jnp.where(live, moved, current),...  11.5 us
    all_to_all x1, starting transfers between devices, gather_in_order(): lax.all_to_all(jnp.stack([tiles] * lax.axis_size(axes[k])), axes[k], 0, 0)  8.6 us
    select_n x5, other arithmetic, tick(): start = jnp.where(index == 0, own, received)  6.64 us
    ppermute x5, starting transfers between devices, shifted(): lax.ppermute(value, axis, [(source, source + steps) for source in range(l...  6.46 us
  transfers between devices with their start and end apart: 6, of which 6 were waited for; matrix products, arithmetic and copies ran while one was open for 4% of the time, Pallas kernels for 0%

profile of v1, /device:TPU:24, one launch (start us, length us, event | category | flops | bytes accessed | tf_op | source)
XLA Modules:
  0.0 274.6 jit_solution(7546250612630975013)
XLA Ops:
  0.9 10.8 %all_to_all.15 = bf16[4,1,2,1,128,128]{5,4,2,3,1,0:T(8,128)(2,1)S(1)} all-to-all(bf16[4,1,2,1,128,128]{5,4,2,3,1,0:T(8,128)(2,1)S(1)} %stack.14), channel_id=1, replica_groups=mesh['energy_0'=8,'energy_1'=4,'energy_2'=2,'sector'=4] {'energy_1'}, dimensions={0} | all-to-all | bytes 524288 | tf_op jit(solution)/shard_map/all_to_all | solution.py:21
  11.7 1.8 stack.15
  13.5 8.6 %all-to-all-start.1 = ((bf16[8,4,2,1,128,128]{5,4,1,2,3,0:T(8,128)(2,1)}), bf16[8,4,2,1,128,128]{5,4,1,2,3,0:T(8,128)(2,1)S(1)}, u32[]{:S(2)}, u32[]{:S(2)}) async-start(bf16[8,4,2,1,128,128]{5,4,1,2,3,0:T(8,128)(2,1)} %stack.15), calls=%async_computation.1 | async-start | bytes 4194304 | tf_op jit(solution)/shard_map/all_to_all | solution.py:21
  22.1 49.8 %all-to-all-done.1 = bf16[8,4,2,1,128,128]{5,4,1,2,3,0:T(8,128)(2,1)S(1)} async-done(((bf16[8,4,2,1,128,128]{5,4,1,2,3,0:T(8,128)(2,1)}), bf16[8,4,2,1,128,128]{5,4,1,2,3,0:T(8,128)(2,1)S(1)}, u32[]{:S(2)}, u32[]{:S(2)}) %all-to-all-start.1) | async-done | bytes 2097184 | tf_op jit(solution)/shard_map/all_to_all | solution.py:21
  73.0 7.1 %all_to_all.16 = bf16[2,32,2,1,128,128]{5,4,1,2,3,0:T(8,128)(2,1)S(1)} all-to-all(bf16[2,32,2,1,128,128]{5,4,1,2,3,0:T(8,128)(2,1)S(1)} %copy.9), channel_id=1, replica_groups=mesh['energy_0'=8,'energy_1'=4,'energy_2'=2,'sector'=4] {'energy_2'}, dimensions={0} | all-to-all | bytes 8388608 | tf_op jit(solution)/shard_map/all_to_all | solution.py:21
  80.5 2.3 copy_multiply_fusion
  82.8 1.5 broadcast_in_dim.13
  84.3 190.3 %while.16 = (s32[]{:T(128)}, f32[1,2,1024,128]{3,2,1,0:T(8,128)S(1)}, f32[2,2,1024,128]{3,2,1,0:T(8,128)}, s32[]{:T(128)}, pred[]{:T(512)}, /*index=5*/f32[2,2,1...) while((s32[]{:T(128)}, ...), condition=%wide.region_3.4_spmd, body=%wide.region_0.3_spmd.sunk | while | flops 2166753280 | bytes 80532288 | solution.py:91
  84.3 1.3 dynamic-slice_select_fusion.2
  85.6 1.3 collective-permute-start
  86.9 2.3 select_dynamic-update-slice_fusion.2
  89.2 23.5 %collective-permute-done = f32[1,2,1024,128]{3,2,1,0:T(8,128)S(1)} collective-permute-done((f32[1,2,1024,128]{3,2,1,0:T(8,128)S(1)}, f32[1,2,1024,128]{3,2,1,0:T(8,128)S(1)}, u32[]{:S(2)}, u32[]{:S(2)}) %collective-permute-start) | collective-permute-done | bytes 1048608 | tf_op jit(solution)/shard_map/while/body/eval_jaxpr/ppermute | solution.py:36
  112.7 1.3 dynamic-slice_select_fusion.2
  114.1 1.3 collective-permute-start
  115.4 2.3 select_dynamic-update-slice_fusion.2
  117.7 22.6 %collective-permute-done = f32[1,2,1024,128]{3,2,1,0:T(8,128)S(1)} collective-permute-done((f32[1,2,1024,128]{3,2,1,0:T(8,128)S(1)}, f32[1,2,1024,128]{3,2,1,0:T(8,128)S(1)}, u32[]{:S(2)}, u32[]{:S(2)}) %collective-permute-start) | collective-permute-done | bytes 1048608 | tf_op jit(solution)/shard_map/while/body/eval_jaxpr/ppermute | solution.py:36
  140.3 1.3 dynamic-slice_select_fusion.2
  141.7 1.3 collective-permute-start
  143.0 2.3 select_dynamic-update-slice_fusion.2
  145.3 53.4 %collective-permute-done = f32[1,2,1024,128]{3,2,1,0:T(8,128)S(1)} collective-permute-done((f32[1,2,1024,128]{3,2,1,0:T(8,128)S(1)}, f32[1,2,1024,128]{3,2,1,0:T(8,128)S(1)}, u32[]{:S(2)}, u32[]{:S(2)}) %collective-permute-start) | collective-permute-done | bytes 1048608 | tf_op jit(solution)/shard_map/while/body/eval_jaxpr/ppermute | solution.py:36
  198.7 1.3 dynamic-slice_select_fusion.2
  200.0 11.7 %conditional.2 = (f32[1,2,1024,128]{3,2,1,0:T(8,128)S(1)}) conditional(s32[]{:T(128)} %convert_element_type.107, f32[1,2,1024,128]{3,2,1,0:T(8,128)S(1)} %dynamic-slice_select_fusion.2, (f32[1,2,1024,128]{3,2,1,0:T(8,128)S(1)}, f32[2]{0:T(128)S(1)}, s32[]{:T(128)}, f32[1024]{0:T(1024)S(1)}, bf16[2,8,8,128,128]{4,3,2,1,0:T(8,128)(2,1)}) %tuple.51), branch_computations={%region_1.1_spmd, %region_2.2_spmd} | conditional | flops 2166228992 | bytes 70045752 | solution.py:82
  202.0 2.5 fusion.14
  211.7 1.3 collective-permute-start
  213.0 2.3 select_dynamic-update-slice_fusion.2
  215.3 21.8 %collective-permute-done = f32[1,2,1024,128]{3,2,1,0:T(8,128)S(1)} collective-permute-done((f32[1,2,1024,128]{3,2,1,0:T(8,128)S(1)}, f32[1,2,1024,128]{3,2,1,0:T(8,128)S(1)}, u32[]{:S(2)}, u32[]{:S(2)}) %collective-permute-start) | collective-permute-done | bytes 1048608 | tf_op jit(solution)/shard_map/while/body/eval_jaxpr/ppermute | solution.py:36
  237.1 1.3 dynamic-slice_select_fusion.2
  238.4 11.7 %conditional.2 = (f32[1,2,1024,128]{3,2,1,0:T(8,128)S(1)}) conditional(s32[]{:T(128)} %convert_element_type.107, f32[1,2,1024,128]{3,2,1,0:T(8,128)S(1)} %dynamic-slice_select_fusion.2, (f32[1,2,1024,128]{3,2,1,0:T(8,128)S(1)}, f32[2]{0:T(128)S(1)}, s32[]{:T(128)}, f32[1024]{0:T(1024)S(1)}, bf16[2,8,8,128,128]{4,3,2,1,0:T(8,128)(2,1)}) %tuple.51), branch_computations={%region_1.1_spmd, %region_2.2_spmd} | conditional | flops 2166228992 | bytes 70045752 | solution.py:82
  240.4 2.4 fusion.14
  250.1 1.3 collective-permute-start
  251.4 2.3 select_dynamic-update-slice_fusion.2
  253.7 20.9 %collective-permute-done = f32[1,2,1024,128]{3,2,1,0:T(8,128)S(1)} collective-permute-done((f32[1,2,1024,128]{3,2,1,0:T(8,128)S(1)}, f32[1,2,1024,128]{3,2,1,0:T(8,128)S(1)}, u32[]{:S(2)}, u32[]{:S(2)}) %collective-permute-start) | collective-permute-done | bytes 1048608 | tf_op jit(solution)/shard_map/while/body/eval_jaxpr/ppermute | solution.py:36
  (52 shorter events, 20.6 us)
Async XLA Ops:
  13.5 8.6 %copy-start.1 = (s32[2,8,8]{2,1,0:T(8,128)S(1)}, s32[2,8,8]{2,1,0:T(8,128)}, u32[]{:S(2)}) copy-start(s32[2,8,8]{2,1,0:T(8,128)} %param.12) | copy-start | bytes 1540
  13.5 8.6 %copy-start.2 = (s32[1024]{0:T(1024)S(1)}, s32[1024]{0:T(1024)}, u32[]{:S(2)}) copy-start(s32[1024]{0:T(1024)} %param.11) | copy-start | bytes 12292
  13.5 58.4 %all-to-all-start.1 = ((bf16[8,4,2,1,128,128]{5,4,1,2,3,0:T(8,128)(2,1)}), bf16[8,4,2,1,128,128]{5,4,1,2,3,0:T(8,128)(2,1)S(1)}, u32[]{:S(2)}, u32[]{:S(2)}) async-start(bf16[8,4,2,1,128,128]{5,4,1,2,3,0:T(8,128)(2,1)} %stack.15), calls=%async_computation.1 | async-start | bytes 4194304 | tf_op jit(solution)/shard_map/all_to_all | solution.py:21
  82.7 1.5 copy-start.3
  85.6 27.1 %collective-permute-start = (f32[1,2,1024,128]{3,2,1,0:T(8,128)S(1)}, f32[1,2,1024,128]{3,2,1,0:T(8,128)S(1)}, u32[]{:S(2)}, u32[]{:S(2)}) collective-permute-start(f32[1,2,1024,128]{3,2,1,0:T(8,128)S(1)} %get-tuple-element.329), channel_id=1, source_target_pairs={{0,1},{1,2},{2,3},{4,5},{5,6},{6,7},{8,9},{9,10},{10,11},{12,13},{... | collective-permute-start | bytes 3145736 | tf_op jit(solution)/shard_map/while/body/eval_jaxpr/ppermute | solution.py:36
  114.1 26.2 %collective-permute-start = (f32[1,2,1024,128]{3,2,1,0:T(8,128)S(1)}, f32[1,2,1024,128]{3,2,1,0:T(8,128)S(1)}, u32[]{:S(2)}, u32[]{:S(2)}) collective-permute-start(f32[1,2,1024,128]{3,2,1,0:T(8,128)S(1)} %get-tuple-element.329), channel_id=1, source_target_pairs={{0,1},{1,2},{2,3},{4,5},{5,6},{6,7},{8,9},{9,10},{10,11},{12,13},{... | collective-permute-start | bytes 3145736 | tf_op jit(solution)/shard_map/while/body/eval_jaxpr/ppermute | solution.py:36
  141.7 57.0 %collective-permute-start = (f32[1,2,1024,128]{3,2,1,0:T(8,128)S(1)}, f32[1,2,1024,128]{3,2,1,0:T(8,128)S(1)}, u32[]{:S(2)}, u32[]{:S(2)}) collective-permute-start(f32[1,2,1024,128]{3,2,1,0:T(8,128)S(1)} %get-tuple-element.329), channel_id=1, source_target_pairs={{0,1},{1,2},{2,3},{4,5},{5,6},{6,7},{8,9},{9,10},{10,11},{12,13},{... | collective-permute-start | bytes 3145736 | tf_op jit(solution)/shard_map/while/body/eval_jaxpr/ppermute | solution.py:36
  202.0 2.8 %copy-start = (bf16[2,8,8,128,128]{4,3,2,1,0:T(8,128)(2,1)S(1)}, bf16[2,8,8,128,128]{4,3,2,1,0:T(8,128)(2,1)}, u32[]{:S(2)}) copy-start(bf16[2,8,8,128,128]{4,3,2,1,0:T(8,128)(2,1)} %get-tuple-element.194) | copy-start | bytes 12582916 | tf_op jit(solution)/shard_map/while/body/eval_jaxpr/cond
  211.7 25.4 %collective-permute-start = (f32[1,2,1024,128]{3,2,1,0:T(8,128)S(1)}, f32[1,2,1024,128]{3,2,1,0:T(8,128)S(1)}, u32[]{:S(2)}, u32[]{:S(2)}) collective-permute-start(f32[1,2,1024,128]{3,2,1,0:T(8,128)S(1)} %get-tuple-element.329), channel_id=1, source_target_pairs={{0,1},{1,2},{2,3},{4,5},{5,6},{6,7},{8,9},{9,10},{10,11},{12,13},{... | collective-permute-start | bytes 3145736 | tf_op jit(solution)/shard_map/while/body/eval_jaxpr/ppermute | solution.py:36
  240.4 2.8 %copy-start = (bf16[2,8,8,128,128]{4,3,2,1,0:T(8,128)(2,1)S(1)}, bf16[2,8,8,128,128]{4,3,2,1,0:T(8,128)(2,1)}, u32[]{:S(2)}) copy-start(bf16[2,8,8,128,128]{4,3,2,1,0:T(8,128)(2,1)} %get-tuple-element.194) | copy-start | bytes 12582916 | tf_op jit(solution)/shard_map/while/body/eval_jaxpr/cond
  250.1 24.5 %collective-permute-start = (f32[1,2,1024,128]{3,2,1,0:T(8,128)S(1)}, f32[1,2,1024,128]{3,2,1,0:T(8,128)S(1)}, u32[]{:S(2)}, u32[]{:S(2)}) collective-permute-start(f32[1,2,1024,128]{3,2,1,0:T(8,128)S(1)} %get-tuple-element.329), channel_id=1, source_target_pairs={{0,1},{1,2},{2,3},{4,5},{5,6},{6,7},{8,9},{9,10},{10,11},{12,13},{... | collective-permute-start | bytes 3145736 | tf_op jit(solution)/shard_map/while/body/eval_jaxpr/ppermute | solution.py:36
